TPU v7x, 512 devices: a whole 4x4x16 slice. The times are simulated.
512 devices in a mesh: req: 16 (over x, y_lo, core), blk: 32 (over z, y_hi).
Axes of the slice: x: 4, y: 4 (y_hi: 2, y_lo: 2; y = y_hi * 2 + y_lo), z: 16, core: 2. Of those that a mesh axis runs over, the one named last changes fastest.
Arguments:
- queries: bfloat16 [16, 32, 512, 512], P('req', 'blk'), may hold values from -6 to 6
- keys: bfloat16 [16, 32, 512, 256], P('req', 'blk'), may hold values from -25 to 25
- values: bfloat16 [16, 32, 512, 256], P('req', 'blk'), may hold values from -6 to 6
- block_map: int32 [16, 8, 2], P('req'), may hold values from 0 to 15, as said below
- lengths: int32 [16], P('req'), may hold values from 1024 to 4096
- group_of_prompt: int32 [16], replicated, may hold values from 0 to 15, each once
- decode_rank: int32 [16, 32], P('req'), may hold values from 0 to 31, as said below
Outputs:
- attended: bfloat16 [16, 32, 512, 512], P('req', 'blk')
- cache: bfloat16 [16, 4096, 2048], P('req', 'blk')
Inputs may be any that keep to these rules, and one draw needn't show every extreme that they name: In each group, block_map[g] holds each of 0 to 15 once, and the two halves of each slot hold blocks b and 15 - b, in either order. `decode_rank`: each group's row holds each of 0 to 31 once.
All inputs are finite; a program needn't handle non-finite values.
Results may differ from a plain program's by a relative error of at most 0.0098.
Values may be sent and summed in bfloat16 or wider, within the bound.
A program may use at most 64 MiB of HBM per device.

v0:
```python
import math
import jax
import jax.numpy as jnp
from jax import lax
from jax.sharding import PartitionSpec as P

QUERY_HEADS = 16
KEY_VALUE_HEADS = 8
HEAD_SIZE = 128
HEAD_DIVISIONS = 4
Q_DEV = 4
KV_DEV = 2
cap_value = 50.0
query_scale = 1.0 / 12.0
rope_base = 10000.0


def shifted(shard, axis, by):
    peers = lax.axis_size(axis)
    return lax.ppermute(shard, axis, [(i, (i + by) % peers) for i in range(peers)])


def apply_rotary(row_block, token_position, head_count):
    row_count = row_block.shape[0]
    head_width = row_block.shape[1] // head_count
    half_width = head_width // 2
    shaped = row_block.astype(jnp.float32).reshape(row_count, head_count, head_width)
    frequency = jnp.exp(
        -math.log(rope_base) * (2.0 * jnp.arange(half_width, dtype=jnp.float32)) / head_width
    )
    angles = token_position.astype(jnp.float32)[:, None] * frequency[None, :]
    cosine = jnp.cos(angles)[:, None, :]
    sine_part = jnp.sin(angles)[:, None, :]
    front_half = shaped[:, :, :half_width]
    second = shaped[:, :, half_width:]
    turned = jnp.concatenate(
        [front_half * cosine - second * sine_part, second * cosine + front_half * sine_part], axis=2
    )
    return turned.reshape(row_count, head_count * head_width)


def slot_positions(table, slot, block_len):
    slot_ids = jnp.arange(table.shape[0], dtype=jnp.int32)
    chosen = jnp.sum(jnp.where((slot_ids == slot)[:, None], table, 0), axis=0)
    return chosen[:, None] * block_len + jnp.arange(block_len, dtype=jnp.int32)[None, :]


def forward_step(buffer):
    return shifted(buffer, "blk", HEAD_DIVISIONS)


def on_device(queries, keys, values, block_map, lengths, group_of_prompt, decode_rank):
    token_rows = queries.shape[2]
    block_len = token_rows // 2
    rank_count = lax.axis_size("blk")
    cache_slot_count = rank_count // HEAD_DIVISIONS
    member = lax.axis_index("blk")
    own_slot = member // HEAD_DIVISIONS
    group_id = lax.axis_index("req")
    group_portion = QUERY_HEADS // KEY_VALUE_HEADS
    kv_dev_width = KV_DEV * HEAD_SIZE
    all_lengths = lax.all_gather(lengths, "req", axis=0, tiled=True)
    length = jnp.sum(jnp.where(group_of_prompt == group_id, all_lengths, 0))
    table = block_map[0]
    own_pos = slot_positions(table, own_slot, block_len)
    flat_pos = own_pos.reshape(-1)
    query_rot = (apply_rotary(queries[0, 0], flat_pos, Q_DEV) * query_scale).astype(jnp.bfloat16)
    rotated_key = apply_rotary(keys[0, 0], flat_pos, KV_DEV).astype(jnp.bfloat16)
    value_row_list = values[0, 0]
    query_halves = query_rot.reshape(2, block_len, KV_DEV, group_portion, HEAD_SIZE)

    def attend_tile(numerator, denominator, portion, key_sub, value_sub, key_pos):
        scores = jnp.einsum(
            "qkgd,nkd->kgqn", query_halves[portion], key_sub, preferred_element_type=jnp.float32
        )
        capped = cap_value * jnp.tanh(scores / cap_value)
        allowed = key_pos[None, :] <= own_pos[portion][:, None]
        expo_vals = jnp.where(allowed[None, None], jnp.exp(capped), 0.0)
        weight = expo_vals.astype(jnp.bfloat16)
        numerator = numerator + jnp.einsum(
            "kgqn,nkd->qkgd", weight, value_sub, preferred_element_type=jnp.float32
        )
        denominator = denominator + jnp.sum(expo_vals, axis=3)
        return (numerator, denominator)

    def absorb(totals, packet, slot):
        numerator, denominator = totals
        key_pos = slot_positions(table, slot, block_len)
        key_blocks = packet[0].reshape(2, block_len, KV_DEV, HEAD_SIZE)
        value_blocks = packet[1].reshape(2, block_len, KV_DEV, HEAD_SIZE)
        new_numer = []
        new_denom = []
        for portion in range(2):
            result_pair = (numerator[portion], denominator[portion])
            for half in range(2):
                result_pair = attend_tile(
                    result_pair[0],
                    result_pair[1],
                    portion,
                    key_blocks[half],
                    value_blocks[half],
                    key_pos[half],
                )
            new_numer.append(result_pair[0])
            new_denom.append(result_pair[1])
        return (jnp.stack(new_numer), jnp.stack(new_denom))

    packet = jnp.stack([rotated_key, value_row_list])
    start_numer = jnp.zeros((2, block_len, KV_DEV, group_portion, HEAD_SIZE), jnp.float32)
    start_denom = jnp.zeros((2, KV_DEV, group_portion, block_len), jnp.float32)
    numerator, denominator = absorb((start_numer, start_denom), packet, own_slot)

    def step_single(turn, carry):
        numer_now, denom_now, buffer = carry
        buffer = forward_step(buffer)
        numer_now, denom_now = absorb(
            (numer_now, denom_now), buffer, (own_slot - turn) % cache_slot_count
        )
        return (numer_now, denom_now, buffer)

    numerator, denominator, _ = lax.fori_loop(
        1, cache_slot_count, step_single, (numerator, denominator, packet)
    )
    safe_denom = jnp.where(denominator > 0.0, denominator, 1.0)
    output = numerator / jnp.transpose(safe_denom, (0, 3, 1, 2))[..., None]
    output = output.reshape(token_rows, Q_DEV * HEAD_SIZE)
    live = flat_pos < length
    attended = jnp.where(live[:, None], output, 0.0).astype(jnp.bfloat16)
    joined = jnp.concatenate([rotated_key, value_row_list], axis=1)
    kept_rows = jnp.where(live[:, None], joined, jnp.zeros_like(joined))
    rank_portion = block_len // rank_count
    shaped = kept_rows.reshape(2, rank_portion, rank_count, 2 * kv_dev_width)
    rank_of = decode_rank[0]
    rank_ids = jnp.arange(rank_count, dtype=jnp.int32)
    inverse = jnp.sum(
        jnp.where(rank_of[None, :] == rank_ids[:, None], rank_ids[None, :], 0), axis=1
    )
    outgoing = jnp.take(shaped, inverse, axis=2)
    arrived = lax.all_to_all(outgoing, "blk", split_axis=2, concat_axis=2, tiled=True)
    regrouped = arrived.reshape(2, rank_portion, cache_slot_count, HEAD_DIVISIONS, 2, kv_dev_width)
    regrouped = jnp.transpose(regrouped, (2, 0, 1, 4, 3, 5)).reshape(
        cache_slot_count * 2 * rank_portion, 2 * KEY_VALUE_HEADS * HEAD_SIZE
    )
    target = (
        table.reshape(-1)[:, None] * rank_portion
        + jnp.arange(rank_portion, dtype=jnp.int32)[None, :]
    )
    cache_rows = (
        jnp.zeros((token_rows // HEAD_DIVISIONS, 2 * KEY_VALUE_HEADS * HEAD_SIZE), jnp.bfloat16)
        .at[target.reshape(-1)]
        .set(regrouped)
    )
    return (attended[None, None], cache_rows[None])


def solution(mesh):
    placed = (
        P("req", "blk", None, None),
        P("req", "blk", None, None),
        P("req", "blk", None, None),
        P("req", None, None),
        P("req"),
        P(),
        P("req", None),
    )
    return jax.shard_map(
        on_device,
        mesh=mesh,
        in_specs=placed,
        out_specs=(P("req", "blk", None, None), P("req", "blk", None)),
        check_vma=False,
    )
```

profile of v0, /device:TPU:16, one launch (start us, length us, event | category | flops | bytes accessed | tf_op | source)
XLA Modules:
  0.0 276.7 jit_solution(10896126467494985319)
XLA Ops:
  0.7 0.6 copy-done.4
  1.5 0.7 copy-done.2
  2.3 1.1 copy.148
  5.4 1.3 dynamic-slice
  6.7 0.8 dynamic-update-slice
  7.4 12.1 %all-reduce = s32[16]{0:T(128)S(1)} all-reduce(s32[16]{0:T(128)S(1)} %dynamic-update-slice), channel_id=1, replica_groups=mesh['req'=16,'blk'=32] {'req'}, use_global_device_ids=true, to_apply=%add | all-reduce | flops 16 | bytes 128
  21.1 0.6 fusion.71
  21.7 0.6 add_compare_fusion
  22.6 0.6 gather_fusion
  23.2 0.9 select_bitcast_fusion
  24.1 18.2 %all-to-all-start = ((bf16[2,8,32,512]{3,1,0,2:T(8,128)(2,1)}), bf16[2,8,32,512]{3,1,0,2:T(8,128)(2,1)S(1)}, u32[]{:S(2)}, u32[]{:S(2)}) async-start(bf16[2,8,32,512]{3,1,0,2:T(8,128)(2,1)} %select_bitcast_fusion), calls=%async_computation | async-start | bytes 1048576 | tf_op jit(solution)/shard_map/all_to_all | solution.py:139
  42.6 0.7 copy-done.1
  48.2 222.1 %while.19 = (s32[]{:T(128)}, f32[2,256,2,2,128]{4,1,3,2,0:T(8,128)S(1)}, f32[2,2,2,256]{3,2,1,0:T(2,128)S(1)}, bf16[2,512,256]{1,2,0:T(8,128)(2,1)S(1)}, s32[]{:...) while((s32[]{:T(128)}, ...), condition=%wide.region_12.13_spmd, body=%wide.region_6.0_spmd.sunk | while | flops 543164992 | bytes 17381768 | solution.py:121
  48.2 4.3 %collective-permute-start = (bf16[2,512,256]{1,2,0:T(8,128)(2,1)S(1)}, bf16[2,512,256]{1,2,0:T(8,128)(2,1)S(1)}, u32[]{:S(2)}, u32[]{:S(2)}) collective-permute-start(bf16[2,512,256]{1,2,0:T(8,128)(2,1)S(1)} %get-tuple-element.428), channel_id=1, source_target_pairs={{0,4},{1,5},{2,6},{3,7},{4,8},{5,9},{6,10},{7,11},{8,12},{9,13},{1... | collective-permute-start | bytes 1572872 | tf_op jit(solution)/shard_map/while/body/eval_jaxpr/ppermute | solution.py:20
  52.9 31.1 %collective-permute-done = bf16[2,512,256]{1,2,0:T(8,128)(2,1)S(1)} collective-permute-done((bf16[2,512,256]{1,2,0:T(8,128)(2,1)S(1)}, bf16[2,512,256]{1,2,0:T(8,128)(2,1)S(1)}, u32[]{:S(2)}, u32[]{:S(2)}) %collective-permute-start) | collective-permute-done | bytes 524320 | tf_op jit(solution)/shard_map/while/body/eval_jaxpr/ppermute | solution.py:20
  84.7 0.5 fusion.152
  87.9 1.9 collective-permute-start
  90.3 17.8 %collective-permute-done = bf16[2,512,256]{1,2,0:T(8,128)(2,1)S(1)} collective-permute-done((bf16[2,512,256]{1,2,0:T(8,128)(2,1)S(1)}, bf16[2,512,256]{1,2,0:T(8,128)(2,1)S(1)}, u32[]{:S(2)}, u32[]{:S(2)}) %collective-permute-start) | collective-permute-done | bytes 524320 | tf_op jit(solution)/shard_map/while/body/eval_jaxpr/ppermute | solution.py:20
  111.9 8.9 %collective-permute-start = (bf16[2,512,256]{1,2,0:T(8,128)(2,1)S(1)}, bf16[2,512,256]{1,2,0:T(8,128)(2,1)S(1)}, u32[]{:S(2)}, u32[]{:S(2)}) collective-permute-start(bf16[2,512,256]{1,2,0:T(8,128)(2,1)S(1)} %get-tuple-element.428), channel_id=1, source_target_pairs={{0,4},{1,5},{2,6},{3,7},{4,8},{5,9},{6,10},{7,11},{8,12},{9,13},{1... | collective-permute-start | bytes 1572872 | tf_op jit(solution)/shard_map/while/body/eval_jaxpr/ppermute | solution.py:20
  121.3 19.4 %collective-permute-done = bf16[2,512,256]{1,2,0:T(8,128)(2,1)S(1)} collective-permute-done((bf16[2,512,256]{1,2,0:T(8,128)(2,1)S(1)}, bf16[2,512,256]{1,2,0:T(8,128)(2,1)S(1)}, u32[]{:S(2)}, u32[]{:S(2)}) %collective-permute-start) | collective-permute-done | bytes 524320 | tf_op jit(solution)/shard_map/while/body/eval_jaxpr/ppermute | solution.py:20
  144.5 8.8 %collective-permute-start = (bf16[2,512,256]{1,2,0:T(8,128)(2,1)S(1)}, bf16[2,512,256]{1,2,0:T(8,128)(2,1)S(1)}, u32[]{:S(2)}, u32[]{:S(2)}) collective-permute-start(bf16[2,512,256]{1,2,0:T(8,128)(2,1)S(1)} %get-tuple-element.428), channel_id=1, source_target_pairs={{0,4},{1,5},{2,6},{3,7},{4,8},{5,9},{6,10},{7,11},{8,12},{9,13},{1... | collective-permute-start | bytes 1572872 | tf_op jit(solution)/shard_map/while/body/eval_jaxpr/ppermute | solution.py:20
  153.8 17.7 %collective-permute-done = bf16[2,512,256]{1,2,0:T(8,128)(2,1)S(1)} collective-permute-done((bf16[2,512,256]{1,2,0:T(8,128)(2,1)S(1)}, bf16[2,512,256]{1,2,0:T(8,128)(2,1)S(1)}, u32[]{:S(2)}, u32[]{:S(2)}) %collective-permute-start) | collective-permute-done | bytes 524320 | tf_op jit(solution)/shard_map/while/body/eval_jaxpr/ppermute | solution.py:20
  175.3 9.2 %collective-permute-start = (bf16[2,512,256]{1,2,0:T(8,128)(2,1)S(1)}, bf16[2,512,256]{1,2,0:T(8,128)(2,1)S(1)}, u32[]{:S(2)}, u32[]{:S(2)}) collective-permute-start(bf16[2,512,256]{1,2,0:T(8,128)(2,1)S(1)} %get-tuple-element.428), channel_id=1, source_target_pairs={{0,4},{1,5},{2,6},{3,7},{4,8},{5,9},{6,10},{7,11},{8,12},{9,13},{1... | collective-permute-start | bytes 1572872 | tf_op jit(solution)/shard_map/while/body/eval_jaxpr/ppermute | solution.py:20
  185.0 21.1 %collective-permute-done = bf16[2,512,256]{1,2,0:T(8,128)(2,1)S(1)} collective-permute-done((bf16[2,512,256]{1,2,0:T(8,128)(2,1)S(1)}, bf16[2,512,256]{1,2,0:T(8,128)(2,1)S(1)}, u32[]{:S(2)}, u32[]{:S(2)}) %collective-permute-start) | collective-permute-done | bytes 524320 | tf_op jit(solution)/shard_map/while/body/eval_jaxpr/ppermute | solution.py:20
  209.9 6.5 %collective-permute-start = (bf16[2,512,256]{1,2,0:T(8,128)(2,1)S(1)}, bf16[2,512,256]{1,2,0:T(8,128)(2,1)S(1)}, u32[]{:S(2)}, u32[]{:S(2)}) collective-permute-start(bf16[2,512,256]{1,2,0:T(8,128)(2,1)S(1)} %get-tuple-element.428), channel_id=1, source_target_pairs={{0,4},{1,5},{2,6},{3,7},{4,8},{5,9},{6,10},{7,11},{8,12},{9,13},{1... | collective-permute-start | bytes 1572872 | tf_op jit(solution)/shard_map/while/body/eval_jaxpr/ppermute | solution.py:20
  216.9 32.6 %collective-permute-done = bf16[2,512,256]{1,2,0:T(8,128)(2,1)S(1)} collective-permute-done((bf16[2,512,256]{1,2,0:T(8,128)(2,1)S(1)}, bf16[2,512,256]{1,2,0:T(8,128)(2,1)S(1)}, u32[]{:S(2)}, u32[]{:S(2)}) %collective-permute-start) | collective-permute-done | bytes 524320 | tf_op jit(solution)/shard_map/while/body/eval_jaxpr/ppermute | solution.py:20
  253.3 5.3 %collective-permute-start = (bf16[2,512,256]{1,2,0:T(8,128)(2,1)S(1)}, bf16[2,512,256]{1,2,0:T(8,128)(2,1)S(1)}, u32[]{:S(2)}, u32[]{:S(2)}) collective-permute-start(bf16[2,512,256]{1,2,0:T(8,128)(2,1)S(1)} %get-tuple-element.428), channel_id=1, source_target_pairs={{0,4},{1,5},{2,6},{3,7},{4,8},{5,9},{6,10},{7,11},{8,12},{9,13},{1... | collective-permute-start | bytes 1572872 | tf_op jit(solution)/shard_map/while/body/eval_jaxpr/ppermute | solution.py:20
  259.1 7.4 %collective-permute-done = bf16[2,512,256]{1,2,0:T(8,128)(2,1)S(1)} collective-permute-done((bf16[2,512,256]{1,2,0:T(8,128)(2,1)S(1)}, bf16[2,512,256]{1,2,0:T(8,128)(2,1)S(1)}, u32[]{:S(2)}, u32[]{:S(2)}) %collective-permute-start) | collective-permute-done | bytes 524320 | tf_op jit(solution)/shard_map/while/body/eval_jaxpr/ppermute | solution.py:20
  271.4 0.6 fusion.70
  272.4 1.0 select_convert_fusion
  273.5 0.7 copy.176
  274.6 2.1 scatter_custom_fusion
  (208 shorter events, 38.6 us)
Async XLA Ops:
  0.7 0.7 copy-start.4
  1.5 0.7 copy-start.2
  4.6 15.0 %copy-start = (bf16[1,1,512,256]{3,2,1,0:T(8,128)(2,1)S(1)}, bf16[1,1,512,256]{3,2,1,0:T(8,128)(2,1)}, u32[]{:S(2)}) copy-start(bf16[1,1,512,256]{3,2,1,0:T(8,128)(2,1)} %param.11) | copy-start | bytes 786436
  20.5 0.7 copy-start.3
  24.1 249.3 %all-to-all-start = ((bf16[2,8,32,512]{3,1,0,2:T(8,128)(2,1)}), bf16[2,8,32,512]{3,1,0,2:T(8,128)(2,1)S(1)}, u32[]{:S(2)}, u32[]{:S(2)}) async-start(bf16[2,8,32,512]{3,1,0,2:T(8,128)(2,1)} %select_bitcast_fusion), calls=%async_computation | async-start | bytes 1048576 | tf_op jit(solution)/shard_map/all_to_all | solution.py:139
  42.3 1.0 copy-start.1
  48.2 35.9 %collective-permute-start = (bf16[2,512,256]{1,2,0:T(8,128)(2,1)S(1)}, bf16[2,512,256]{1,2,0:T(8,128)(2,1)S(1)}, u32[]{:S(2)}, u32[]{:S(2)}) collective-permute-start(bf16[2,512,256]{1,2,0:T(8,128)(2,1)S(1)} %get-tuple-element.428), channel_id=1, source_target_pairs={{0,4},{1,5},{2,6},{3,7},{4,8},{5,9},{6,10},{7,11},{8,12},{9,13},{1... | collective-permute-start | bytes 1572872 | tf_op jit(solution)/shard_map/while/body/eval_jaxpr/ppermute | solution.py:20
  87.9 20.2 %collective-permute-start = (bf16[2,512,256]{1,2,0:T(8,128)(2,1)S(1)}, bf16[2,512,256]{1,2,0:T(8,128)(2,1)S(1)}, u32[]{:S(2)}, u32[]{:S(2)}) collective-permute-start(bf16[2,512,256]{1,2,0:T(8,128)(2,1)S(1)} %get-tuple-element.428), channel_id=1, source_target_pairs={{0,4},{1,5},{2,6},{3,7},{4,8},{5,9},{6,10},{7,11},{8,12},{9,13},{1... | collective-permute-start | bytes 1572872 | tf_op jit(solution)/shard_map/while/body/eval_jaxpr/ppermute | solution.py:20
  111.9 28.8 %collective-permute-start = (bf16[2,512,256]{1,2,0:T(8,128)(2,1)S(1)}, bf16[2,512,256]{1,2,0:T(8,128)(2,1)S(1)}, u32[]{:S(2)}, u32[]{:S(2)}) collective-permute-start(bf16[2,512,256]{1,2,0:T(8,128)(2,1)S(1)} %get-tuple-element.428), channel_id=1, source_target_pairs={{0,4},{1,5},{2,6},{3,7},{4,8},{5,9},{6,10},{7,11},{8,12},{9,13},{1... | collective-permute-start | bytes 1572872 | tf_op jit(solution)/shard_map/while/body/eval_jaxpr/ppermute | solution.py:20
  144.5 27.0 %collective-permute-start = (bf16[2,512,256]{1,2,0:T(8,128)(2,1)S(1)}, bf16[2,512,256]{1,2,0:T(8,128)(2,1)S(1)}, u32[]{:S(2)}, u32[]{:S(2)}) collective-permute-start(bf16[2,512,256]{1,2,0:T(8,128)(2,1)S(1)} %get-tuple-element.428), channel_id=1, source_target_pairs={{0,4},{1,5},{2,6},{3,7},{4,8},{5,9},{6,10},{7,11},{8,12},{9,13},{1... | collective-permute-start | bytes 1572872 | tf_op jit(solution)/shard_map/while/body/eval_jaxpr/ppermute | solution.py:20
  175.3 30.8 %collective-permute-start = (bf16[2,512,256]{1,2,0:T(8,128)(2,1)S(1)}, bf16[2,512,256]{1,2,0:T(8,128)(2,1)S(1)}, u32[]{:S(2)}, u32[]{:S(2)}) collective-permute-start(bf16[2,512,256]{1,2,0:T(8,128)(2,1)S(1)} %get-tuple-element.428), channel_id=1, source_target_pairs={{0,4},{1,5},{2,6},{3,7},{4,8},{5,9},{6,10},{7,11},{8,12},{9,13},{1... | collective-permute-start | bytes 1572872 | tf_op jit(solution)/shard_map/while/body/eval_jaxpr/ppermute | solution.py:20
  209.9 39.7 %collective-permute-start = (bf16[2,512,256]{1,2,0:T(8,128)(2,1)S(1)}, bf16[2,512,256]{1,2,0:T(8,128)(2,1)S(1)}, u32[]{:S(2)}, u32[]{:S(2)}) collective-permute-start(bf16[2,512,256]{1,2,0:T(8,128)(2,1)S(1)} %get-tuple-element.428), channel_id=1, source_target_pairs={{0,4},{1,5},{2,6},{3,7},{4,8},{5,9},{6,10},{7,11},{8,12},{9,13},{1... | collective-permute-start | bytes 1572872 | tf_op jit(solution)/shard_map/while/body/eval_jaxpr/ppermute | solution.py:20
  253.3 13.2 %collective-permute-start = (bf16[2,512,256]{1,2,0:T(8,128)(2,1)S(1)}, bf16[2,512,256]{1,2,0:T(8,128)(2,1)S(1)}, u32[]{:S(2)}, u32[]{:S(2)}) collective-permute-start(bf16[2,512,256]{1,2,0:T(8,128)(2,1)S(1)} %get-tuple-element.428), channel_id=1, source_target_pairs={{0,4},{1,5},{2,6},{3,7},{4,8},{5,9},{6,10},{7,11},{8,12},{9,13},{1... | collective-permute-start | bytes 1572872 | tf_op jit(solution)/shard_map/while/body/eval_jaxpr/ppermute | solution.py:20
where the time goes:
time: 277 us
  waiting for transfers between devices  147 us (53%)
  starting transfers between devices  63.2 us (23%)
  matrix products  28.1 us (10%)
  local copies, waits for them, and re-layouts  13.5 us (5%)
  blocking collectives  12.1 us (4%)
  other arithmetic  9.92 us (4%)
    ppermute x7, waiting for transfers between devices, shifted(): lax.ppermute(shard, axis, [(i, (i + by) % peers) for i in range(peers)])  147 us
    ppermute x7, starting transfers between devices, shifted(): lax.ppermute(shard, axis, [(i, (i + by) % peers) for i in range(peers)])  45 us
    all_to_all x1, starting transfers between devices, on_device(): lax.all_to_all(outgoing, 'blk', split_axis=2, concat_axis=2, tiled=True)  18.2 us
    dot_general x32, matrix products, attend_tile(): jnp.einsum('qkgd,nkd->kgqn', query_halves[portion], key_sub, preferred_el...  17 us
    unnamed x1, blocking collectives  12.1 us
    dot_general x32, matrix products, attend_tile(): jnp.einsum('kgqn,nkd->qkgd', weight, value_sub, preferred_element_type=jn...  11.1 us
    unnamed x19, local copies, waits for them, and re-layouts  6.42 us
  transfers between devices with their start and end apart: 8, of which 7 were waited for; matrix products, arithmetic and copies ran while one was open for 13% of the time, Pallas kernels for 0%

commit v1 on v0

--- a/solution.py
+++ b/solution.py
@@ -136,7 +136,10 @@
         jnp.where(rank_of[None, :] == rank_ids[:, None], rank_ids[None, :], 0), axis=1
     )
     outgoing = jnp.take(shaped, inverse, axis=2)
-    arrived = lax.all_to_all(outgoing, "blk", split_axis=2, concat_axis=2, tiled=True)
+    arrived = jnp.concatenate(
+        lax.all_to_all(jnp.stack(jnp.split(outgoing, lax.axis_size("blk"), axis=2)), "blk", 0, 0),
+        axis=2,
+    )
     regrouped = arrived.reshape(2, rank_portion, cache_slot_count, HEAD_DIVISIONS, 2, kv_dev_width)
     regrouped = jnp.transpose(regrouped, (2, 0, 1, 4, 3, 5)).reshape(
         cache_slot_count * 2 * rank_portion, 2 * KEY_VALUE_HEADS * HEAD_SIZE

time: 277 us -> 296 us (1.069)
  the two profiles are of different devices: /device:TPU:16 before, /device:TPU:130 now
where the time goes in v1:
time: 296 us; the launch traced here: 295 us
  waiting for transfers between devices  149 us (50%)
  starting transfers between devices  62.1 us (21%)
  local copies, waits for them, and re-layouts  32.9 us (11%)
  matrix products  28.1 us (9%)
  blocking collectives  11.1 us (4%)
  other arithmetic  9.12 us (3%)
    ppermute x7, waiting for transfers between devices, shifted(): lax.ppermute(shard, axis, [(i, (i + by) % peers) for i in range(peers)])  149 us
    ppermute x7, starting transfers between devices, shifted(): lax.ppermute(shard, axis, [(i, (i + by) % peers) for i in range(peers)])  45.7 us
    unnamed x50, local copies, waits for them, and re-layouts  25.2 us
    dot_general x32, matrix products, attend_tile(): jnp.einsum('qkgd,nkd->kgqn', query_halves[portion], key_sub, preferred_el...  17 us
    all_to_all x1, starting transfers between devices, on_device(): lax.all_to_all(jnp.stack(jnp.split(outgoing, lax.axis_size('blk'), axis=2...  16.3 us
    unnamed x1, blocking collectives  11.1 us
    dot_general x32, matrix products, attend_tile(): jnp.einsum('kgqn,nkd->qkgd', weight, value_sub, preferred_element_type=jn...  11.1 us
  transfers between devices with their start and end apart: 8, of which 7 were waited for; matrix products, arithmetic and copies ran while one was open for 13% of the time, Pallas kernels for 0%

profile of v1, /device:TPU:130, one launch (start us, length us, event | category | flops | bytes accessed | tf_op | source)
XLA Modules:
  0.0 295.3 jit_solution(10119930460342370033)
XLA Ops:
  0.7 0.6 copy-done.4
  1.5 0.7 copy-done.2
  2.3 1.1 copy.179
  5.4 1.3 dynamic-slice
  6.7 0.8 dynamic-update-slice
  7.4 11.1 %all-reduce = s32[16]{0:T(128)S(1)} all-reduce(s32[16]{0:T(128)S(1)} %dynamic-update-slice), channel_id=1, replica_groups=mesh['req'=16,'blk'=32] {'req'}, use_global_device_ids=true, to_apply=%add | all-reduce | flops 16 | bytes 128
  20.1 0.6 fusion.71
  20.8 0.6 add_compare_fusion
  22.3 0.6 constant_dynamic-update-slice_fusion.31
  24.1 0.6 constant_dynamic-update-slice_fusion.28
  24.7 0.6 constant_dynamic-update-slice_fusion.27
  41.7 16.3 %all-to-all-start = ((bf16[32,2,8,1,512]{4,2,1,3,0:T(8,128)(2,1)}), bf16[32,2,8,1,512]{4,2,1,3,0:T(8,128)(2,1)S(1)}, u32[]{:S(2)}, u32[]{:S(2)}) async-start(bf16[32,2,8,1,512]{4,2,1,3,0:T(8,128)(2,1)} %constant_dynamic-update-slice_fusion), calls=%async_computation | async-start | bytes 1048576 | tf_op jit(solution)/shard_map/all_to_all | solution.py:140
  58.4 0.7 copy-done.1
  63.9 224.9 %while.19 = (s32[]{:T(128)}, f32[2,256,2,2,128]{4,1,3,2,0:T(8,128)S(1)}, f32[2,2,2,256]{3,2,1,0:T(2,128)S(1)}, bf16[2,512,256]{1,2,0:T(8,128)(2,1)S(1)}, s32[]{:...) while((s32[]{:T(128)}, ...), condition=%wide.region_12.13_spmd, body=%wide.region_6.0_spmd.sunk | while | flops 543164992 | bytes 17381768 | solution.py:121
  63.9 4.3 %collective-permute-start = (bf16[2,512,256]{1,2,0:T(8,128)(2,1)S(1)}, bf16[2,512,256]{1,2,0:T(8,128)(2,1)S(1)}, u32[]{:S(2)}, u32[]{:S(2)}) collective-permute-start(bf16[2,512,256]{1,2,0:T(8,128)(2,1)S(1)} %get-tuple-element.428), channel_id=1, source_target_pairs={{0,4},{1,5},{2,6},{3,7},{4,8},{5,9},{6,10},{7,11},{8,12},{9,13},{1... | collective-permute-start | bytes 1572872 | tf_op jit(solution)/shard_map/while/body/eval_jaxpr/ppermute | solution.py:20
  68.7 28.3 %collective-permute-done = bf16[2,512,256]{1,2,0:T(8,128)(2,1)S(1)} collective-permute-done((bf16[2,512,256]{1,2,0:T(8,128)(2,1)S(1)}, bf16[2,512,256]{1,2,0:T(8,128)(2,1)S(1)}, u32[]{:S(2)}, u32[]{:S(2)}) %collective-permute-start) | collective-permute-done | bytes 524320 | tf_op jit(solution)/shard_map/while/body/eval_jaxpr/ppermute | solution.py:20
  100.7 4.3 %collective-permute-start = (bf16[2,512,256]{1,2,0:T(8,128)(2,1)S(1)}, bf16[2,512,256]{1,2,0:T(8,128)(2,1)S(1)}, u32[]{:S(2)}, u32[]{:S(2)}) collective-permute-start(bf16[2,512,256]{1,2,0:T(8,128)(2,1)S(1)} %get-tuple-element.428), channel_id=1, source_target_pairs={{0,4},{1,5},{2,6},{3,7},{4,8},{5,9},{6,10},{7,11},{8,12},{9,13},{1... | collective-permute-start | bytes 1572872 | tf_op jit(solution)/shard_map/while/body/eval_jaxpr/ppermute | solution.py:20
  105.5 12.6 %collective-permute-done = bf16[2,512,256]{1,2,0:T(8,128)(2,1)S(1)} collective-permute-done((bf16[2,512,256]{1,2,0:T(8,128)(2,1)S(1)}, bf16[2,512,256]{1,2,0:T(8,128)(2,1)S(1)}, u32[]{:S(2)}, u32[]{:S(2)}) %collective-permute-start) | collective-permute-done | bytes 524320 | tf_op jit(solution)/shard_map/while/body/eval_jaxpr/ppermute | solution.py:20
  121.9 14.7 %collective-permute-start = (bf16[2,512,256]{1,2,0:T(8,128)(2,1)S(1)}, bf16[2,512,256]{1,2,0:T(8,128)(2,1)S(1)}, u32[]{:S(2)}, u32[]{:S(2)}) collective-permute-start(bf16[2,512,256]{1,2,0:T(8,128)(2,1)S(1)} %get-tuple-element.428), channel_id=1, source_target_pairs={{0,4},{1,5},{2,6},{3,7},{4,8},{5,9},{6,10},{7,11},{8,12},{9,13},{1... | collective-permute-start | bytes 1572872 | tf_op jit(solution)/shard_map/while/body/eval_jaxpr/ppermute | solution.py:20
  137.1 21.2 %collective-permute-done = bf16[2,512,256]{1,2,0:T(8,128)(2,1)S(1)} collective-permute-done((bf16[2,512,256]{1,2,0:T(8,128)(2,1)S(1)}, bf16[2,512,256]{1,2,0:T(8,128)(2,1)S(1)}, u32[]{:S(2)}, u32[]{:S(2)}) %collective-permute-start) | collective-permute-done | bytes 524320 | tf_op jit(solution)/shard_map/while/body/eval_jaxpr/ppermute | solution.py:20
  162.0 6.5 %collective-permute-start = (bf16[2,512,256]{1,2,0:T(8,128)(2,1)S(1)}, bf16[2,512,256]{1,2,0:T(8,128)(2,1)S(1)}, u32[]{:S(2)}, u32[]{:S(2)}) collective-permute-start(bf16[2,512,256]{1,2,0:T(8,128)(2,1)S(1)} %get-tuple-element.428), channel_id=1, source_target_pairs={{0,4},{1,5},{2,6},{3,7},{4,8},{5,9},{6,10},{7,11},{8,12},{9,13},{1... | collective-permute-start | bytes 1572872 | tf_op jit(solution)/shard_map/while/body/eval_jaxpr/ppermute | solution.py:20
  169.0 31.8 %collective-permute-done = bf16[2,512,256]{1,2,0:T(8,128)(2,1)S(1)} collective-permute-done((bf16[2,512,256]{1,2,0:T(8,128)(2,1)S(1)}, bf16[2,512,256]{1,2,0:T(8,128)(2,1)S(1)}, u32[]{:S(2)}, u32[]{:S(2)}) %collective-permute-start) | collective-permute-done | bytes 524320 | tf_op jit(solution)/shard_map/while/body/eval_jaxpr/ppermute | solution.py:20
  204.6 8.8 %collective-permute-start = (bf16[2,512,256]{1,2,0:T(8,128)(2,1)S(1)}, bf16[2,512,256]{1,2,0:T(8,128)(2,1)S(1)}, u32[]{:S(2)}, u32[]{:S(2)}) collective-permute-start(bf16[2,512,256]{1,2,0:T(8,128)(2,1)S(1)} %get-tuple-element.428), channel_id=1, source_target_pairs={{0,4},{1,5},{2,6},{3,7},{4,8},{5,9},{6,10},{7,11},{8,12},{9,13},{1... | collective-permute-start | bytes 1572872 | tf_op jit(solution)/shard_map/while/body/eval_jaxpr/ppermute | solution.py:20
  213.8 21.7 %collective-permute-done = bf16[2,512,256]{1,2,0:T(8,128)(2,1)S(1)} collective-permute-done((bf16[2,512,256]{1,2,0:T(8,128)(2,1)S(1)}, bf16[2,512,256]{1,2,0:T(8,128)(2,1)S(1)}, u32[]{:S(2)}, u32[]{:S(2)}) %collective-permute-start) | collective-permute-done | bytes 524320 | tf_op jit(solution)/shard_map/while/body/eval_jaxpr/ppermute | solution.py:20
  239.3 5.3 %collective-permute-start = (bf16[2,512,256]{1,2,0:T(8,128)(2,1)S(1)}, bf16[2,512,256]{1,2,0:T(8,128)(2,1)S(1)}, u32[]{:S(2)}, u32[]{:S(2)}) collective-permute-start(bf16[2,512,256]{1,2,0:T(8,128)(2,1)S(1)} %get-tuple-element.428), channel_id=1, source_target_pairs={{0,4},{1,5},{2,6},{3,7},{4,8},{5,9},{6,10},{7,11},{8,12},{9,13},{1... | collective-permute-start | bytes 1572872 | tf_op jit(solution)/shard_map/while/body/eval_jaxpr/ppermute | solution.py:20
  245.1 23.0 %collective-permute-done = bf16[2,512,256]{1,2,0:T(8,128)(2,1)S(1)} collective-permute-done((bf16[2,512,256]{1,2,0:T(8,128)(2,1)S(1)}, bf16[2,512,256]{1,2,0:T(8,128)(2,1)S(1)}, u32[]{:S(2)}, u32[]{:S(2)}) %collective-permute-start) | collective-permute-done | bytes 524320 | tf_op jit(solution)/shard_map/while/body/eval_jaxpr/ppermute | solution.py:20
  271.8 1.9 collective-permute-start
  274.3 10.8 %collective-permute-done = bf16[2,512,256]{1,2,0:T(8,128)(2,1)S(1)} collective-permute-done((bf16[2,512,256]{1,2,0:T(8,128)(2,1)S(1)}, bf16[2,512,256]{1,2,0:T(8,128)(2,1)S(1)}, u32[]{:S(2)}, u32[]{:S(2)}) %collective-permute-start) | collective-permute-done | bytes 524320 | tf_op jit(solution)/shard_map/while/body/eval_jaxpr/ppermute | solution.py:20
  289.9 0.6 fusion.70
  290.9 1.0 select_convert_fusion
  292.0 0.7 copy.207
  293.1 2.1 scatter_custom_fusion
  (240 shorter events, 57.4 us)
Async XLA Ops:
  0.7 0.7 copy-start.4
  1.5 0.7 copy-start.2
  4.6 14.0 %copy-start = (bf16[1,1,512,256]{3,2,1,0:T(8,128)(2,1)S(1)}, bf16[1,1,512,256]{3,2,1,0:T(8,128)(2,1)}, u32[]{:S(2)}) copy-start(bf16[1,1,512,256]{3,2,1,0:T(8,128)(2,1)} %param.11) | copy-start | bytes 786436
  19.5 0.7 copy-start.3
  41.7 250.2 %all-to-all-start = ((bf16[32,2,8,1,512]{4,2,1,3,0:T(8,128)(2,1)}), bf16[32,2,8,1,512]{4,2,1,3,0:T(8,128)(2,1)S(1)}, u32[]{:S(2)}, u32[]{:S(2)}) async-start(bf16[32,2,8,1,512]{4,2,1,3,0:T(8,128)(2,1)} %constant_dynamic-update-slice_fusion), calls=%async_computation | async-start | bytes 1048576 | tf_op jit(solution)/shard_map/all_to_all | solution.py:140
  58.1 1.0 copy-start.1
  63.9 33.0 %collective-permute-start = (bf16[2,512,256]{1,2,0:T(8,128)(2,1)S(1)}, bf16[2,512,256]{1,2,0:T(8,128)(2,1)S(1)}, u32[]{:S(2)}, u32[]{:S(2)}) collective-permute-start(bf16[2,512,256]{1,2,0:T(8,128)(2,1)S(1)} %get-tuple-element.428), channel_id=1, source_target_pairs={{0,4},{1,5},{2,6},{3,7},{4,8},{5,9},{6,10},{7,11},{8,12},{9,13},{1... | collective-permute-start | bytes 1572872 | tf_op jit(solution)/shard_map/while/body/eval_jaxpr/ppermute | solution.py:20
  100.7 17.3 %collective-permute-start = (bf16[2,512,256]{1,2,0:T(8,128)(2,1)S(1)}, bf16[2,512,256]{1,2,0:T(8,128)(2,1)S(1)}, u32[]{:S(2)}, u32[]{:S(2)}) collective-permute-start(bf16[2,512,256]{1,2,0:T(8,128)(2,1)S(1)} %get-tuple-element.428), channel_id=1, source_target_pairs={{0,4},{1,5},{2,6},{3,7},{4,8},{5,9},{6,10},{7,11},{8,12},{9,13},{1... | collective-permute-start | bytes 1572872 | tf_op jit(solution)/shard_map/while/body/eval_jaxpr/ppermute | solution.py:20
  121.9 36.4 %collective-permute-start = (bf16[2,512,256]{1,2,0:T(8,128)(2,1)S(1)}, bf16[2,512,256]{1,2,0:T(8,128)(2,1)S(1)}, u32[]{:S(2)}, u32[]{:S(2)}) collective-permute-start(bf16[2,512,256]{1,2,0:T(8,128)(2,1)S(1)} %get-tuple-element.428), channel_id=1, source_target_pairs={{0,4},{1,5},{2,6},{3,7},{4,8},{5,9},{6,10},{7,11},{8,12},{9,13},{1... | collective-permute-start | bytes 1572872 | tf_op jit(solution)/shard_map/while/body/eval_jaxpr/ppermute | solution.py:20
  162.0 38.7 %collective-permute-start = (bf16[2,512,256]{1,2,0:T(8,128)(2,1)S(1)}, bf16[2,512,256]{1,2,0:T(8,128)(2,1)S(1)}, u32[]{:S(2)}, u32[]{:S(2)}) collective-permute-start(bf16[2,512,256]{1,2,0:T(8,128)(2,1)S(1)} %get-tuple-element.428), channel_id=1, source_target_pairs={{0,4},{1,5},{2,6},{3,7},{4,8},{5,9},{6,10},{7,11},{8,12},{9,13},{1... | collective-permute-start | bytes 1572872 | tf_op jit(solution)/shard_map/while/body/eval_jaxpr/ppermute | solution.py:20
  204.6 31.0 %collective-permute-start = (bf16[2,512,256]{1,2,0:T(8,128)(2,1)S(1)}, bf16[2,512,256]{1,2,0:T(8,128)(2,1)S(1)}, u32[]{:S(2)}, u32[]{:S(2)}) collective-permute-start(bf16[2,512,256]{1,2,0:T(8,128)(2,1)S(1)} %get-tuple-element.428), channel_id=1, source_target_pairs={{0,4},{1,5},{2,6},{3,7},{4,8},{5,9},{6,10},{7,11},{8,12},{9,13},{1... | collective-permute-start | bytes 1572872 | tf_op jit(solution)/shard_map/while/body/eval_jaxpr/ppermute | solution.py:20
  239.3 28.7 %collective-permute-start = (bf16[2,512,256]{1,2,0:T(8,128)(2,1)S(1)}, bf16[2,512,256]{1,2,0:T(8,128)(2,1)S(1)}, u32[]{:S(2)}, u32[]{:S(2)}) collective-permute-start(bf16[2,512,256]{1,2,0:T(8,128)(2,1)S(1)} %get-tuple-element.428), channel_id=1, source_target_pairs={{0,4},{1,5},{2,6},{3,7},{4,8},{5,9},{6,10},{7,11},{8,12},{9,13},{1... | collective-permute-start | bytes 1572872 | tf_op jit(solution)/shard_map/while/body/eval_jaxpr/ppermute | solution.py:20
  271.8 13.2 %collective-permute-start = (bf16[2,512,256]{1,2,0:T(8,128)(2,1)S(1)}, bf16[2,512,256]{1,2,0:T(8,128)(2,1)S(1)}, u32[]{:S(2)}, u32[]{:S(2)}) collective-permute-start(bf16[2,512,256]{1,2,0:T(8,128)(2,1)S(1)} %get-tuple-element.428), channel_id=1, source_target_pairs={{0,4},{1,5},{2,6},{3,7},{4,8},{5,9},{6,10},{7,11},{8,12},{9,13},{1... | collective-permute-start | bytes 1572872 | tf_op jit(solution)/shard_map/while/body/eval_jaxpr/ppermute | solution.py:20
